TPU v7x, 32 devices: a whole 2x2x4 slice. The times are simulated.
32 devices in a mesh: blk: 8 (over z, y), rhs: 4 (over x, core).
Axes of the slice: x: 2, y: 2, z: 4, core: 2. Of those that a mesh axis runs over, the one named last changes fastest.
Arguments:
- rhs: float32 [8, 8, 8, 256, 128], P(None, None, 'blk', 'rhs'), parts along dimension 3, may hold values from -6 to 6
- lower_tiles: bfloat16 [8, 8, 8, 3, 128, 128], P(None, None, 'blk'), may hold values from -0.25 to 0.25
- lower_block_columns: int32 [8, 8, 8, 3], P(None, None, 'blk'), may hold values from 0 to 511, as said below
- upper_tiles: bfloat16 [8, 8, 8, 3, 128, 128], P(None, None, 'blk'), may hold values from -0.25 to 0.25
- upper_cols: int32 [8, 8, 8, 3], P(None, None, 'blk'), may hold values from 0 to 511, as said below
- diag_inverse: bfloat16 [8, 8, 8, 128, 128], P(None, None, 'blk')
Outputs:
- solution: bfloat16 [8, 8, 8, 256, 128], P(None, None, 'blk', 'rhs'), parts along dimension 3
There are 4 independent parts, one for each index of `rhs`. A program takes and returns all parts, laid end to end along the dimension named above; an argument that names none is the same for every part. Nothing has to cross between parts.
Inputs may be any that keep to these rules, and one draw needn't show every extreme that they name: `lower_block_columns`: entry k of block row (l * 8 + m) * 8 + p is either that row's own number (an empty slot) or ((l - 1) * 8 + m) * 8 + (p + d) mod 8 with d one of -1, 0, 1; the nonempty slots of a row have distinct d; rows with l = 0 have only empty slots. `upper_cols`: entry k of block row (l * 8 + m) * 8 + p is either that row's own number (an empty slot) or ((l + 1) * 8 + m) * 8 + (p + d) mod 8 with d one of -1, 0, 1; the nonempty slots of a row have distinct d; rows with l = 7 have only empty slots.
All inputs are finite; a program needn't handle non-finite values.
Results may differ from a plain program's by a relative error of at most 0.015.
Values may be sent and summed in bfloat16 or wider, within the bound.
A program may use at most 64 MiB of HBM per device.

v0:
```python
import jax
import jax.numpy as jnp
from jax import lax
from jax.sharding import PartitionSpec as P


def extended(block, sides, width):
    for axis, dim in sides:
        count = lax.axis_size(axis)
        forward = [(i, i + 1) for i in range(count - 1)]
        forward.append((count - 1, 0))
        backward = [(target, source) for source, target in forward]
        low = lax.ppermute(
            lax.slice_in_dim(block, block.shape[dim] - width, None, axis=dim), axis, forward
        )
        high = lax.ppermute(lax.slice_in_dim(block, 0, width, axis=dim), axis, backward)
        block = jnp.concatenate([low, block, high], axis=dim)
    return block


def row_numbers(level_id, row_count, cycle_size, home_spot):
    return (level_id * row_count + jnp.arange(row_count, dtype=jnp.int32)) * cycle_size + home_spot


def select_terms(
    window, halo_width, shift_amount_value, tile_collection, columns, numbers, cycle_size
):
    home_spot = (numbers % cycle_size)[:, None]
    distance = (columns % cycle_size - home_spot) % cycle_size
    offset_step = jnp.where(distance == 1, 1, jnp.where(distance == cycle_size - 1, -1, 0))
    source = offset_step + (shift_amount_value + halo_width)
    present = columns != numbers[:, None]
    places = jnp.arange(2 * halo_width + 1, dtype=jnp.int32)
    select = ((source[:, :, None] == places) & present[:, :, None]).astype(jnp.bfloat16)
    chosen_entries = jnp.einsum(
        "mkw,wmsb->mksb", select, window, preferred_element_type=jnp.float32
    ).astype(jnp.bfloat16)
    return jnp.einsum(
        "lqfp,lqcp->lfc", chosen_entries, tile_collection, preferred_element_type=jnp.float32
    )


def apply_inverse(summed_terms, inverted_tile_matrix):
    return jnp.einsum(
        "vdj,voj->vdo", summed_terms, inverted_tile_matrix, preferred_element_type=jnp.float32
    ).astype(jnp.bfloat16)


def on_device(rhs, lower_tiles, lower_block_columns, upper_tiles, upper_cols, diag_inverse):
    cycle_size = lax.axis_size("blk")
    position = lax.axis_index("blk")
    level_count = rhs.shape[0]
    row_count = rhs.shape[1]
    sides_in = rhs[:, :, 0]
    lower_tile_group = lower_tiles[:, :, 0]
    lower_index = lower_block_columns[:, :, 0]
    upper_set = upper_tiles[:, :, 0]
    upper_index = upper_cols[:, :, 0]
    inverse = diag_inverse[:, :, 0]
    level_ids = jnp.arange(level_count, dtype=jnp.int32)

    def forward(previous, inputs):
        tile_collection, columns, side_rows, level_id = inputs
        window = extended(previous[None], (("blk", 0),), 1)
        numbers = row_numbers(level_id, row_count, cycle_size, position)
        products = select_terms(window, 1, 0, tile_collection, columns, numbers, cycle_size)
        solved_now = (side_rows - products).astype(jnp.bfloat16)
        return (solved_now, solved_now)

    first_level = sides_in[0].astype(jnp.bfloat16)
    unused, later_levels = lax.scan(
        forward, first_level, (lower_tile_group[1:], lower_index[1:], sides_in[1:], level_ids[1:])
    )
    solved = jnp.concatenate([first_level[None], later_levels], axis=0)
    top_level = apply_inverse(solved[-1], inverse[-1])

    def backward(next_level, inputs):
        tile_collection, columns, inverted_tile_matrix, forward_rows, level_id = inputs
        window = extended(next_level[None], (("blk", 0),), 1)
        numbers = row_numbers(level_id, row_count, cycle_size, position)
        products = select_terms(window, 1, 0, tile_collection, columns, numbers, cycle_size)
        summed_terms = (forward_rows.astype(jnp.float32) - products).astype(jnp.bfloat16)
        solved_now = apply_inverse(summed_terms, inverted_tile_matrix)
        return (solved_now, solved_now)

    unused, lower_levels = lax.scan(
        backward,
        top_level,
        (upper_set[:-1], upper_index[:-1], inverse[:-1], solved[:-1], level_ids[:-1]),
        reverse=True,
    )
    result = jnp.concatenate([lower_levels, top_level[None]], axis=0)
    return result[:, :, None]


def solution(mesh):
    return jax.shard_map(
        on_device,
        mesh=mesh,
        in_specs=(
            P(None, None, "blk", "rhs", None),
            P(None, None, "blk", None, None, None),
            P(None, None, "blk", None),
            P(None, None, "blk", None, None, None),
            P(None, None, "blk", None),
            P(None, None, "blk", None, None),
        ),
        out_specs=P(None, None, "blk", "rhs", None),
        check_vma=False,
    )
```

profile of v0, /device:TPU:0, one launch (start us, length us, event | category | flops | bytes accessed | tf_op | source)
XLA Modules:
  0.0 171.8 jit_solution(13380194208408825122)
XLA Ops:
  1.0 7.4 %slice_bitcast_fusion.1 = bf16[7,8,3,128,128]{4,3,2,1,0:T(8,128)(2,1)} fusion(bf16[8,8,1,3,128,128]{5,4,3,1,0,2:T(8,128)(2,1)} %bitcast.140), kind=kLoop, calls=%fused_computation.71 | loop fusion | bytes 11010048 | tf_op jit(solution)/shard_map/slice | solution.py:72
  9.4 77.1 %while.30 = (s32[]{:T(128)}, bf16[8,64,128]{2,1,0:T(8,128)(2,1)S(1)}, bf16[7,8,64,128]{3,2,1,0:T(8,128)(2,1)S(1)}, f32[7,8,64,128]{3,2,1,0:T(8,128)S(1)}, s32[7,...) while((s32[]{:T(128)}, ...), condition=%wide.region_1.2_spmd, body=%wide.region_0.1_spmd.sunk | while | flops 52036536 | bytes 4458501 | solution.py:71
  9.4 6.1 %collective-permute-start = (bf16[1,8,64,128]{3,2,1,0:T(8,128)(2,1)S(1)}, bf16[1,8,64,128]{3,2,1,0:T(8,128)(2,1)S(1)}, u32[]{:S(2)}, u32[]{:S(2)}) collective-permute-start(bf16[1,8,64,128]{3,2,1,0:T(8,128)(2,1)S(1)} %bitcast.142), channel_id=1, source_target_pairs={{4,0},{8,4},{12,8},{16,12},{20,16},{24,20},{28,24},{0,28},{5,1},{9... | collective-permute-start | bytes 393224 | tf_op jit(solution)/shard_map/while/body/eval_jaxpr/ppermute | solution.py:16
  18.2 4.9 %collective-permute-done.1 = bf16[1,8,64,128]{3,2,1,0:T(8,128)(2,1)S(1)} collective-permute-done((bf16[1,8,64,128]{3,2,1,0:T(8,128)(2,1)S(1)}, bf16[1,8,64,128]{3,2,1,0:T(8,128)(2,1)S(1)}, u32[]{:S(2)}, u32[]{:S(2)}) %collective-permute-start.1) | collective-permute-done | bytes 131104 | tf_op jit(solution)/shard_map/while/body/eval_jaxpr/ppermute | solution.py:13
  28.9 2.9 %collective-permute-done = bf16[1,8,64,128]{3,2,1,0:T(8,128)(2,1)S(1)} collective-permute-done((bf16[1,8,64,128]{3,2,1,0:T(8,128)(2,1)S(1)}, bf16[1,8,64,128]{3,2,1,0:T(8,128)(2,1)S(1)}, u32[]{:S(2)}, u32[]{:S(2)}) %collective-permute-start) | collective-permute-done | bytes 131104 | tf_op jit(solution)/shard_map/while/body/eval_jaxpr/ppermute | solution.py:16
  41.5 2.6 %collective-permute-done.1 = bf16[1,8,64,128]{3,2,1,0:T(8,128)(2,1)S(1)} collective-permute-done((bf16[1,8,64,128]{3,2,1,0:T(8,128)(2,1)S(1)}, bf16[1,8,64,128]{3,2,1,0:T(8,128)(2,1)S(1)}, u32[]{:S(2)}, u32[]{:S(2)}) %collective-permute-start.1) | collective-permute-done | bytes 131104 | tf_op jit(solution)/shard_map/while/body/eval_jaxpr/ppermute | solution.py:13
  46.4 2.0 %collective-permute-start.1 = (bf16[1,8,64,128]{3,2,1,0:T(8,128)(2,1)S(1)}, bf16[1,8,64,128]{3,2,1,0:T(8,128)(2,1)S(1)}, u32[]{:S(2)}, u32[]{:S(2)}) collective-permute-start(bf16[1,8,64,128]{3,2,1,0:T(8,128)(2,1)S(1)} %bitcast.143), channel_id=1, source_target_pairs={{0,4},{4,8},{8,12},{12,16},{16,20},{20,24},{24,28},{28,0},{1,5},{5... | collective-permute-start | bytes 393224 | tf_op jit(solution)/shard_map/while/body/eval_jaxpr/ppermute | solution.py:13
  51.3 2.8 %collective-permute-done.1 = bf16[1,8,64,128]{3,2,1,0:T(8,128)(2,1)S(1)} collective-permute-done((bf16[1,8,64,128]{3,2,1,0:T(8,128)(2,1)S(1)}, bf16[1,8,64,128]{3,2,1,0:T(8,128)(2,1)S(1)}, u32[]{:S(2)}, u32[]{:S(2)}) %collective-permute-start.1) | collective-permute-done | bytes 131104 | tf_op jit(solution)/shard_map/while/body/eval_jaxpr/ppermute | solution.py:13
  59.9 2.2 %collective-permute-done = bf16[1,8,64,128]{3,2,1,0:T(8,128)(2,1)S(1)} collective-permute-done((bf16[1,8,64,128]{3,2,1,0:T(8,128)(2,1)S(1)}, bf16[1,8,64,128]{3,2,1,0:T(8,128)(2,1)S(1)}, u32[]{:S(2)}, u32[]{:S(2)}) %collective-permute-start) | collective-permute-done | bytes 131104 | tf_op jit(solution)/shard_map/while/body/eval_jaxpr/ppermute | solution.py:16
  69.9 2.3 %collective-permute-done = bf16[1,8,64,128]{3,2,1,0:T(8,128)(2,1)S(1)} collective-permute-done((bf16[1,8,64,128]{3,2,1,0:T(8,128)(2,1)S(1)}, bf16[1,8,64,128]{3,2,1,0:T(8,128)(2,1)S(1)}, u32[]{:S(2)}, u32[]{:S(2)}) %collective-permute-start) | collective-permute-done | bytes 131104 | tf_op jit(solution)/shard_map/while/body/eval_jaxpr/ppermute | solution.py:16
  72.2 2.1 %collective-permute-done.1 = bf16[1,8,64,128]{3,2,1,0:T(8,128)(2,1)S(1)} collective-permute-done((bf16[1,8,64,128]{3,2,1,0:T(8,128)(2,1)S(1)}, bf16[1,8,64,128]{3,2,1,0:T(8,128)(2,1)S(1)}, u32[]{:S(2)}, u32[]{:S(2)}) %collective-permute-start.1) | collective-permute-done | bytes 131104 | tf_op jit(solution)/shard_map/while/body/eval_jaxpr/ppermute | solution.py:13
  81.6 2.7 %collective-permute-done.1 = bf16[1,8,64,128]{3,2,1,0:T(8,128)(2,1)S(1)} collective-permute-done((bf16[1,8,64,128]{3,2,1,0:T(8,128)(2,1)S(1)}, bf16[1,8,64,128]{3,2,1,0:T(8,128)(2,1)S(1)}, u32[]{:S(2)}, u32[]{:S(2)}) %collective-permute-start.1) | collective-permute-done | bytes 131104 | tf_op jit(solution)/shard_map/while/body/eval_jaxpr/ppermute | solution.py:13
  88.8 7.4 %slice_bitcast_fusion = bf16[7,8,3,128,128]{4,3,2,1,0:T(8,128)(2,1)} fusion(bf16[8,8,1,3,128,128]{5,4,3,1,0,2:T(8,128)(2,1)} %bitcast.141), kind=kLoop, calls=%fused_computation.70 | loop fusion | bytes 11010048 | tf_op jit(solution)/shard_map/slice | solution.py:89
  97.7 73.0 %while.31 = (s32[]{:T(128)}, bf16[8,64,128]{2,1,0:T(8,128)(2,1)S(1)}, bf16[7,8,64,128]{3,2,1,0:T(8,128)(2,1)S(1)}, bf16[7,8,64,128]{3,2,1,0:T(8,128)(2,1)}, s32[...) while((s32[]{:T(128)}, ...), condition=%wide.region_3.4_spmd, body=%wide.region_2.3_spmd.sunk | while | flops 68944824 | bytes 4590617 | solution.py:86
  102.7 2.8 %collective-permute-done.3 = bf16[1,8,64,128]{3,2,1,0:T(8,128)(2,1)S(1)} collective-permute-done((bf16[1,8,64,128]{3,2,1,0:T(8,128)(2,1)S(1)}, bf16[1,8,64,128]{3,2,1,0:T(8,128)(2,1)S(1)}, u32[]{:S(2)}, u32[]{:S(2)}) %collective-permute-start.3) | collective-permute-done | bytes 131104 | tf_op jit(solution)/shard_map/while/body/eval_jaxpr/ppermute | solution.py:13
  112.9 2.8 %collective-permute-done.3 = bf16[1,8,64,128]{3,2,1,0:T(8,128)(2,1)S(1)} collective-permute-done((bf16[1,8,64,128]{3,2,1,0:T(8,128)(2,1)S(1)}, bf16[1,8,64,128]{3,2,1,0:T(8,128)(2,1)S(1)}, u32[]{:S(2)}, u32[]{:S(2)}) %collective-permute-start.3) | collective-permute-done | bytes 131104 | tf_op jit(solution)/shard_map/while/body/eval_jaxpr/ppermute | solution.py:13
  123.1 2.8 %collective-permute-done.3 = bf16[1,8,64,128]{3,2,1,0:T(8,128)(2,1)S(1)} collective-permute-done((bf16[1,8,64,128]{3,2,1,0:T(8,128)(2,1)S(1)}, bf16[1,8,64,128]{3,2,1,0:T(8,128)(2,1)S(1)}, u32[]{:S(2)}, u32[]{:S(2)}) %collective-permute-start.3) | collective-permute-done | bytes 131104 | tf_op jit(solution)/shard_map/while/body/eval_jaxpr/ppermute | solution.py:13
  133.3 2.9 %collective-permute-done.3 = bf16[1,8,64,128]{3,2,1,0:T(8,128)(2,1)S(1)} collective-permute-done((bf16[1,8,64,128]{3,2,1,0:T(8,128)(2,1)S(1)}, bf16[1,8,64,128]{3,2,1,0:T(8,128)(2,1)S(1)}, u32[]{:S(2)}, u32[]{:S(2)}) %collective-permute-start.3) | collective-permute-done | bytes 131104 | tf_op jit(solution)/shard_map/while/body/eval_jaxpr/ppermute | solution.py:13
  138.6 2.2 %collective-permute-start.3 = (bf16[1,8,64,128]{3,2,1,0:T(8,128)(2,1)S(1)}, bf16[1,8,64,128]{3,2,1,0:T(8,128)(2,1)S(1)}, u32[]{:S(2)}, u32[]{:S(2)}) collective-permute-start(bf16[1,8,64,128]{3,2,1,0:T(8,128)(2,1)S(1)} %bitcast.147), channel_id=1, source_target_pairs={{0,4},{4,8},{8,12},{12,16},{16,20},{20,24},{24,28},{28,0},{1,5},{5... | collective-permute-start | bytes 393224 | tf_op jit(solution)/shard_map/while/body/eval_jaxpr/ppermute | solution.py:13
  143.6 3.3 %collective-permute-done.3 = bf16[1,8,64,128]{3,2,1,0:T(8,128)(2,1)S(1)} collective-permute-done((bf16[1,8,64,128]{3,2,1,0:T(8,128)(2,1)S(1)}, bf16[1,8,64,128]{3,2,1,0:T(8,128)(2,1)S(1)}, u32[]{:S(2)}, u32[]{:S(2)}) %collective-permute-start.3) | collective-permute-done | bytes 131104 | tf_op jit(solution)/shard_map/while/body/eval_jaxpr/ppermute | solution.py:13
  149.3 2.5 %collective-permute-start.3 = (bf16[1,8,64,128]{3,2,1,0:T(8,128)(2,1)S(1)}, bf16[1,8,64,128]{3,2,1,0:T(8,128)(2,1)S(1)}, u32[]{:S(2)}, u32[]{:S(2)}) collective-permute-start(bf16[1,8,64,128]{3,2,1,0:T(8,128)(2,1)S(1)} %bitcast.147), channel_id=1, source_target_pairs={{0,4},{4,8},{8,12},{12,16},{16,20},{20,24},{24,28},{28,0},{1,5},{5... | collective-permute-start | bytes 393224 | tf_op jit(solution)/shard_map/while/body/eval_jaxpr/ppermute | solution.py:13
  154.7 3.5 %collective-permute-done.3 = bf16[1,8,64,128]{3,2,1,0:T(8,128)(2,1)S(1)} collective-permute-done((bf16[1,8,64,128]{3,2,1,0:T(8,128)(2,1)S(1)}, bf16[1,8,64,128]{3,2,1,0:T(8,128)(2,1)S(1)}, u32[]{:S(2)}, u32[]{:S(2)}) %collective-permute-start.3) | collective-permute-done | bytes 131104 | tf_op jit(solution)/shard_map/while/body/eval_jaxpr/ppermute | solution.py:13
  160.6 2.5 %collective-permute-start.3 = (bf16[1,8,64,128]{3,2,1,0:T(8,128)(2,1)S(1)}, bf16[1,8,64,128]{3,2,1,0:T(8,128)(2,1)S(1)}, u32[]{:S(2)}, u32[]{:S(2)}) collective-permute-start(bf16[1,8,64,128]{3,2,1,0:T(8,128)(2,1)S(1)} %bitcast.147), channel_id=1, source_target_pairs={{0,4},{4,8},{8,12},{12,16},{16,20},{20,24},{24,28},{28,0},{1,5},{5... | collective-permute-start | bytes 393224 | tf_op jit(solution)/shard_map/while/body/eval_jaxpr/ppermute | solution.py:13
  166.0 2.3 %collective-permute-done.3 = bf16[1,8,64,128]{3,2,1,0:T(8,128)(2,1)S(1)} collective-permute-done((bf16[1,8,64,128]{3,2,1,0:T(8,128)(2,1)S(1)}, bf16[1,8,64,128]{3,2,1,0:T(8,128)(2,1)S(1)}, u32[]{:S(2)}, u32[]{:S(2)}) %collective-permute-start.3) | collective-permute-done | bytes 131104 | tf_op jit(solution)/shard_map/while/body/eval_jaxpr/ppermute | solution.py:13
  (189 shorter events, 89.5 us)
Async XLA Ops:
  9.4 8.8 %collective-permute-start = (bf16[1,8,64,128]{3,2,1,0:T(8,128)(2,1)S(1)}, bf16[1,8,64,128]{3,2,1,0:T(8,128)(2,1)S(1)}, u32[]{:S(2)}, u32[]{:S(2)}) collective-permute-start(bf16[1,8,64,128]{3,2,1,0:T(8,128)(2,1)S(1)} %bitcast.142), channel_id=1, source_target_pairs={{4,0},{8,4},{12,8},{16,12},{20,16},{24,20},{28,24},{0,28},{5,1},{9... | collective-permute-start | bytes 393224 | tf_op jit(solution)/shard_map/while/body/eval_jaxpr/ppermute | solution.py:16
  15.5 7.7 %collective-permute-start.1 = (bf16[1,8,64,128]{3,2,1,0:T(8,128)(2,1)S(1)}, bf16[1,8,64,128]{3,2,1,0:T(8,128)(2,1)S(1)}, u32[]{:S(2)}, u32[]{:S(2)}) collective-permute-start(bf16[1,8,64,128]{3,2,1,0:T(8,128)(2,1)S(1)} %bitcast.143), channel_id=1, source_target_pairs={{0,4},{4,8},{8,12},{12,16},{16,20},{20,24},{24,28},{28,0},{1,5},{5... | collective-permute-start | bytes 393224 | tf_op jit(solution)/shard_map/while/body/eval_jaxpr/ppermute | solution.py:13
  25.4 6.4 %collective-permute-start = (bf16[1,8,64,128]{3,2,1,0:T(8,128)(2,1)S(1)}, bf16[1,8,64,128]{3,2,1,0:T(8,128)(2,1)S(1)}, u32[]{:S(2)}, u32[]{:S(2)}) collective-permute-start(bf16[1,8,64,128]{3,2,1,0:T(8,128)(2,1)S(1)} %bitcast.142), channel_id=1, source_target_pairs={{4,0},{8,4},{12,8},{16,12},{20,16},{24,20},{28,24},{0,28},{5,1},{9... | collective-permute-start | bytes 393224 | tf_op jit(solution)/shard_map/while/body/eval_jaxpr/ppermute | solution.py:16
  26.1 7.7 %collective-permute-start.1 = (bf16[1,8,64,128]{3,2,1,0:T(8,128)(2,1)S(1)}, bf16[1,8,64,128]{3,2,1,0:T(8,128)(2,1)S(1)}, u32[]{:S(2)}, u32[]{:S(2)}) collective-permute-start(bf16[1,8,64,128]{3,2,1,0:T(8,128)(2,1)S(1)} %bitcast.143), channel_id=1, source_target_pairs={{0,4},{4,8},{8,12},{12,16},{16,20},{20,24},{24,28},{28,0},{1,5},{5... | collective-permute-start | bytes 393224 | tf_op jit(solution)/shard_map/while/body/eval_jaxpr/ppermute | solution.py:13
  36.0 5.5 %collective-permute-start = (bf16[1,8,64,128]{3,2,1,0:T(8,128)(2,1)S(1)}, bf16[1,8,64,128]{3,2,1,0:T(8,128)(2,1)S(1)}, u32[]{:S(2)}, u32[]{:S(2)}) collective-permute-start(bf16[1,8,64,128]{3,2,1,0:T(8,128)(2,1)S(1)} %bitcast.142), channel_id=1, source_target_pairs={{4,0},{8,4},{12,8},{16,12},{20,16},{24,20},{28,24},{0,28},{5,1},{9... | collective-permute-start | bytes 393224 | tf_op jit(solution)/shard_map/while/body/eval_jaxpr/ppermute | solution.py:16
  36.4 7.7 %collective-permute-start.1 = (bf16[1,8,64,128]{3,2,1,0:T(8,128)(2,1)S(1)}, bf16[1,8,64,128]{3,2,1,0:T(8,128)(2,1)S(1)}, u32[]{:S(2)}, u32[]{:S(2)}) collective-permute-start(bf16[1,8,64,128]{3,2,1,0:T(8,128)(2,1)S(1)} %bitcast.143), channel_id=1, source_target_pairs={{0,4},{4,8},{8,12},{12,16},{16,20},{20,24},{24,28},{28,0},{1,5},{5... | collective-permute-start | bytes 393224 | tf_op jit(solution)/shard_map/while/body/eval_jaxpr/ppermute | solution.py:13
  46.3 5.0 %collective-permute-start = (bf16[1,8,64,128]{3,2,1,0:T(8,128)(2,1)S(1)}, bf16[1,8,64,128]{3,2,1,0:T(8,128)(2,1)S(1)}, u32[]{:S(2)}, u32[]{:S(2)}) collective-permute-start(bf16[1,8,64,128]{3,2,1,0:T(8,128)(2,1)S(1)} %bitcast.142), channel_id=1, source_target_pairs={{4,0},{8,4},{12,8},{16,12},{20,16},{24,20},{28,24},{0,28},{5,1},{9... | collective-permute-start | bytes 393224 | tf_op jit(solution)/shard_map/while/body/eval_jaxpr/ppermute | solution.py:16
  46.4 7.7 %collective-permute-start.1 = (bf16[1,8,64,128]{3,2,1,0:T(8,128)(2,1)S(1)}, bf16[1,8,64,128]{3,2,1,0:T(8,128)(2,1)S(1)}, u32[]{:S(2)}, u32[]{:S(2)}) collective-permute-start(bf16[1,8,64,128]{3,2,1,0:T(8,128)(2,1)S(1)} %bitcast.143), channel_id=1, source_target_pairs={{0,4},{4,8},{8,12},{12,16},{16,20},{20,24},{24,28},{28,0},{1,5},{5... | collective-permute-start | bytes 393224 | tf_op jit(solution)/shard_map/while/body/eval_jaxpr/ppermute | solution.py:13
  56.3 5.8 %collective-permute-start = (bf16[1,8,64,128]{3,2,1,0:T(8,128)(2,1)S(1)}, bf16[1,8,64,128]{3,2,1,0:T(8,128)(2,1)S(1)}, u32[]{:S(2)}, u32[]{:S(2)}) collective-permute-start(bf16[1,8,64,128]{3,2,1,0:T(8,128)(2,1)S(1)} %bitcast.142), channel_id=1, source_target_pairs={{4,0},{8,4},{12,8},{16,12},{20,16},{24,20},{28,24},{0,28},{5,1},{9... | collective-permute-start | bytes 393224 | tf_op jit(solution)/shard_map/while/body/eval_jaxpr/ppermute | solution.py:16
  56.4 7.7 %collective-permute-start.1 = (bf16[1,8,64,128]{3,2,1,0:T(8,128)(2,1)S(1)}, bf16[1,8,64,128]{3,2,1,0:T(8,128)(2,1)S(1)}, u32[]{:S(2)}, u32[]{:S(2)}) collective-permute-start(bf16[1,8,64,128]{3,2,1,0:T(8,128)(2,1)S(1)} %bitcast.143), channel_id=1, source_target_pairs={{0,4},{4,8},{8,12},{12,16},{16,20},{20,24},{24,28},{28,0},{1,5},{5... | collective-permute-start | bytes 393224 | tf_op jit(solution)/shard_map/while/body/eval_jaxpr/ppermute | solution.py:13
  66.3 5.8 %collective-permute-start = (bf16[1,8,64,128]{3,2,1,0:T(8,128)(2,1)S(1)}, bf16[1,8,64,128]{3,2,1,0:T(8,128)(2,1)S(1)}, u32[]{:S(2)}, u32[]{:S(2)}) collective-permute-start(bf16[1,8,64,128]{3,2,1,0:T(8,128)(2,1)S(1)} %bitcast.142), channel_id=1, source_target_pairs={{4,0},{8,4},{12,8},{16,12},{20,16},{24,20},{28,24},{0,28},{5,1},{9... | collective-permute-start | bytes 393224 | tf_op jit(solution)/shard_map/while/body/eval_jaxpr/ppermute | solution.py:16
  66.6 7.7 %collective-permute-start.1 = (bf16[1,8,64,128]{3,2,1,0:T(8,128)(2,1)S(1)}, bf16[1,8,64,128]{3,2,1,0:T(8,128)(2,1)S(1)}, u32[]{:S(2)}, u32[]{:S(2)}) collective-permute-start(bf16[1,8,64,128]{3,2,1,0:T(8,128)(2,1)S(1)} %bitcast.143), channel_id=1, source_target_pairs={{0,4},{4,8},{8,12},{12,16},{16,20},{20,24},{24,28},{28,0},{1,5},{5... | collective-permute-start | bytes 393224 | tf_op jit(solution)/shard_map/while/body/eval_jaxpr/ppermute | solution.py:13
  76.5 5.1 %collective-permute-start = (bf16[1,8,64,128]{3,2,1,0:T(8,128)(2,1)S(1)}, bf16[1,8,64,128]{3,2,1,0:T(8,128)(2,1)S(1)}, u32[]{:S(2)}, u32[]{:S(2)}) collective-permute-start(bf16[1,8,64,128]{3,2,1,0:T(8,128)(2,1)S(1)} %bitcast.142), channel_id=1, source_target_pairs={{4,0},{8,4},{12,8},{16,12},{20,16},{24,20},{28,24},{0,28},{5,1},{9... | collective-permute-start | bytes 393224 | tf_op jit(solution)/shard_map/while/body/eval_jaxpr/ppermute | solution.py:16
  76.6 7.7 %collective-permute-start.1 = (bf16[1,8,64,128]{3,2,1,0:T(8,128)(2,1)S(1)}, bf16[1,8,64,128]{3,2,1,0:T(8,128)(2,1)S(1)}, u32[]{:S(2)}, u32[]{:S(2)}) collective-permute-start(bf16[1,8,64,128]{3,2,1,0:T(8,128)(2,1)S(1)} %bitcast.143), channel_id=1, source_target_pairs={{0,4},{4,8},{8,12},{12,16},{16,20},{20,24},{24,28},{28,0},{1,5},{5... | collective-permute-start | bytes 393224 | tf_op jit(solution)/shard_map/while/body/eval_jaxpr/ppermute | solution.py:13
  97.8 7.7 %collective-permute-start.3 = (bf16[1,8,64,128]{3,2,1,0:T(8,128)(2,1)S(1)}, bf16[1,8,64,128]{3,2,1,0:T(8,128)(2,1)S(1)}, u32[]{:S(2)}, u32[]{:S(2)}) collective-permute-start(bf16[1,8,64,128]{3,2,1,0:T(8,128)(2,1)S(1)} %bitcast.147), channel_id=1, source_target_pairs={{0,4},{4,8},{8,12},{12,16},{16,20},{20,24},{24,28},{28,0},{1,5},{5... | collective-permute-start | bytes 393224 | tf_op jit(solution)/shard_map/while/body/eval_jaxpr/ppermute | solution.py:13
  107.9 7.7 %collective-permute-start.3 = (bf16[1,8,64,128]{3,2,1,0:T(8,128)(2,1)S(1)}, bf16[1,8,64,128]{3,2,1,0:T(8,128)(2,1)S(1)}, u32[]{:S(2)}, u32[]{:S(2)}) collective-permute-start(bf16[1,8,64,128]{3,2,1,0:T(8,128)(2,1)S(1)} %bitcast.147), channel_id=1, source_target_pairs={{0,4},{4,8},{8,12},{12,16},{16,20},{20,24},{24,28},{28,0},{1,5},{5... | collective-permute-start | bytes 393224 | tf_op jit(solution)/shard_map/while/body/eval_jaxpr/ppermute | solution.py:13
  118.1 7.8 %collective-permute-start.3 = (bf16[1,8,64,128]{3,2,1,0:T(8,128)(2,1)S(1)}, bf16[1,8,64,128]{3,2,1,0:T(8,128)(2,1)S(1)}, u32[]{:S(2)}, u32[]{:S(2)}) collective-permute-start(bf16[1,8,64,128]{3,2,1,0:T(8,128)(2,1)S(1)} %bitcast.147), channel_id=1, source_target_pairs={{0,4},{4,8},{8,12},{12,16},{16,20},{20,24},{24,28},{28,0},{1,5},{5... | collective-permute-start | bytes 393224 | tf_op jit(solution)/shard_map/while/body/eval_jaxpr/ppermute | solution.py:13
  128.3 7.8 %collective-permute-start.3 = (bf16[1,8,64,128]{3,2,1,0:T(8,128)(2,1)S(1)}, bf16[1,8,64,128]{3,2,1,0:T(8,128)(2,1)S(1)}, u32[]{:S(2)}, u32[]{:S(2)}) collective-permute-start(bf16[1,8,64,128]{3,2,1,0:T(8,128)(2,1)S(1)} %bitcast.147), channel_id=1, source_target_pairs={{0,4},{4,8},{8,12},{12,16},{16,20},{20,24},{24,28},{28,0},{1,5},{5... | collective-permute-start | bytes 393224 | tf_op jit(solution)/shard_map/while/body/eval_jaxpr/ppermute | solution.py:13
  138.5 5.1 %collective-permute-start.2 = (bf16[1,8,64,128]{3,2,1,0:T(8,128)(2,1)S(1)}, bf16[1,8,64,128]{3,2,1,0:T(8,128)(2,1)S(1)}, u32[]{:S(2)}, u32[]{:S(2)}) collective-permute-start(bf16[1,8,64,128]{3,2,1,0:T(8,128)(2,1)S(1)} %bitcast.146), channel_id=1, source_target_pairs={{4,0},{8,4},{12,8},{16,12},{20,16},{24,20},{28,24},{0,28},{5,1},{9... | collective-permute-start | bytes 393224 | tf_op jit(solution)/shard_map/while/body/eval_jaxpr/ppermute | solution.py:16
  138.6 8.3 %collective-permute-start.3 = (bf16[1,8,64,128]{3,2,1,0:T(8,128)(2,1)S(1)}, bf16[1,8,64,128]{3,2,1,0:T(8,128)(2,1)S(1)}, u32[]{:S(2)}, u32[]{:S(2)}) collective-permute-start(bf16[1,8,64,128]{3,2,1,0:T(8,128)(2,1)S(1)} %bitcast.147), channel_id=1, source_target_pairs={{0,4},{4,8},{8,12},{12,16},{16,20},{20,24},{24,28},{28,0},{1,5},{5... | collective-permute-start | bytes 393224 | tf_op jit(solution)/shard_map/while/body/eval_jaxpr/ppermute | solution.py:13
  149.2 5.5 %collective-permute-start.2 = (bf16[1,8,64,128]{3,2,1,0:T(8,128)(2,1)S(1)}, bf16[1,8,64,128]{3,2,1,0:T(8,128)(2,1)S(1)}, u32[]{:S(2)}, u32[]{:S(2)}) collective-permute-start(bf16[1,8,64,128]{3,2,1,0:T(8,128)(2,1)S(1)} %bitcast.146), channel_id=1, source_target_pairs={{4,0},{8,4},{12,8},{16,12},{20,16},{24,20},{28,24},{0,28},{5,1},{9... | collective-permute-start | bytes 393224 | tf_op jit(solution)/shard_map/while/body/eval_jaxpr/ppermute | solution.py:16
  149.3 8.9 %collective-permute-start.3 = (bf16[1,8,64,128]{3,2,1,0:T(8,128)(2,1)S(1)}, bf16[1,8,64,128]{3,2,1,0:T(8,128)(2,1)S(1)}, u32[]{:S(2)}, u32[]{:S(2)}) collective-permute-start(bf16[1,8,64,128]{3,2,1,0:T(8,128)(2,1)S(1)} %bitcast.147), channel_id=1, source_target_pairs={{0,4},{4,8},{8,12},{12,16},{16,20},{20,24},{24,28},{28,0},{1,5},{5... | collective-permute-start | bytes 393224 | tf_op jit(solution)/shard_map/while/body/eval_jaxpr/ppermute | solution.py:13
  160.6 5.5 %collective-permute-start.2 = (bf16[1,8,64,128]{3,2,1,0:T(8,128)(2,1)S(1)}, bf16[1,8,64,128]{3,2,1,0:T(8,128)(2,1)S(1)}, u32[]{:S(2)}, u32[]{:S(2)}) collective-permute-start(bf16[1,8,64,128]{3,2,1,0:T(8,128)(2,1)S(1)} %bitcast.146), channel_id=1, source_target_pairs={{4,0},{8,4},{12,8},{16,12},{20,16},{24,20},{28,24},{0,28},{5,1},{9... | collective-permute-start | bytes 393224 | tf_op jit(solution)/shard_map/while/body/eval_jaxpr/ppermute | solution.py:16
  160.6 7.7 %collective-permute-start.3 = (bf16[1,8,64,128]{3,2,1,0:T(8,128)(2,1)S(1)}, bf16[1,8,64,128]{3,2,1,0:T(8,128)(2,1)S(1)}, u32[]{:S(2)}, u32[]{:S(2)}) collective-permute-start(bf16[1,8,64,128]{3,2,1,0:T(8,128)(2,1)S(1)} %bitcast.147), channel_id=1, source_target_pairs={{0,4},{4,8},{8,12},{12,16},{16,20},{20,24},{24,28},{28,0},{1,5},{5... | collective-permute-start | bytes 393224 | tf_op jit(solution)/shard_map/while/body/eval_jaxpr/ppermute | solution.py:13
  (11 other events, 118.2 us)
where the time goes:
time: 173 us; the launch traced here: 172 us
  waiting for transfers between devices  53.7 us (31%)
  starting transfers between devices  34.2 us (20%)
  matrix products  32.4 us (19%)
  local copies, waits for them, and re-layouts  29.2 us (17%)
  other arithmetic  12.7 us (7%)
  loops' own time  9.5 us (5%)
    ppermute x14, waiting for transfers between devices, extended(): lax.ppermute(lax.slice_in_dim(block, block.shape[dim] - width, None, axis...  39.2 us
    ppermute x14, starting transfers between devices, extended(): lax.ppermute(lax.slice_in_dim(block, block.shape[dim] - width, None, axis...  26.2 us
    ppermute x14, waiting for transfers between devices, extended(): lax.ppermute(lax.slice_in_dim(block, 0, width, axis=dim), axis, backward)  14.5 us
    dot_general x8, matrix products, apply_inverse(): jnp.einsum('vdj,voj->vdo', summed_terms, inverted_tile_matrix, preferred_...  13.7 us
    dot_general x7, matrix products, select_terms(): jnp.einsum('lqfp,lqcp->lfc', chosen_entries, tile_collection, preferred_e...  11.5 us
    dynamic_slice x14, local copies, waits for them, and re-layouts, on_device(): lax.scan(forward, first_level, (lower_tile_group[1:], lower_index[1:], si...  8.38 us
    ppermute x14, starting transfers between devices, extended(): lax.ppermute(lax.slice_in_dim(block, 0, width, axis=dim), axis, backward)  8.05 us
    slice x1, local copies, waits for them, and re-layouts, on_device(): lower_tile_group[1:]  7.37 us
  transfers between devices with their start and end apart: 28, of which 27 were waited for; matrix products, arithmetic and copies ran while one was open for 12% of the time, Pallas kernels for 0%

commit v1 on v0

v1 whole, which is shorter than its diff:
```python
import functools

import jax
import jax.numpy as jnp
from jax import lax
from jax.experimental import pallas as pl
from jax.experimental.pallas import tpu as pltpu
from jax.sharding import PartitionSpec as P

MESH = pl.DeviceIdType.MESH
CHUNKS = 4


def product(x, tile):
    return lax.dot_general(x, tile, (((1,), (1,)), ((), ())), preferred_element_type=jnp.float32)


def sweep_kernel(
    n,
    chunks,
    lower_cols,
    upper_cols,
    rhs,
    lower,
    upper,
    inverse,
    out,
    rhs_v,
    lower_v,
    upper_v,
    inverse_v,
    y,
    x,
    from_left,
    from_right,
    load_sem,
    store_sem,
    send_sem,
    recv_sem,
):
    levels, rows, sides, block = rhs.shape
    slots = lower.shape[2]
    step = rows // chunks
    me = lax.axis_index("blk")
    left = lax.rem(me + n - 1, n)
    right = lax.rem(me + 1, n)

    def load(kind, level):
        source, target = ((rhs, rhs_v), (lower, lower_v), (upper, upper_v), (inverse, inverse_v))[kind]
        return pltpu.make_async_copy(source.at[level], target.at[level], load_sem.at[kind, level])

    def start_forward(level, carry):
        load(0, level).start()
        load(1, level).start()
        return carry

    def start_backward(i, carry):
        level = levels - 2 - i
        load(3, level).start()
        load(2, level).start()
        return carry

    load(0, 0).start()
    barrier = pltpu.get_barrier_semaphore()
    for neighbour in (left, right):
        pl.semaphore_signal(barrier, inc=1, device_id={"blk": neighbour}, device_id_type=MESH)
    lax.fori_loop(1, levels, start_forward, 0)
    load(3, levels - 1).start()
    lax.fori_loop(0, levels - 1, start_backward, 0)

    def exchange(source, sweep, level, c):
        part = pl.ds(c * step, step)
        to_right = pltpu.make_async_remote_copy(
            src_ref=source.at[level, part],
            dst_ref=from_left.at[sweep, level, part],
            send_sem=send_sem.at[sweep, level, c, 0],
            recv_sem=recv_sem.at[sweep, level, c, 0],
            device_id={"blk": right},
            device_id_type=MESH,
        )
        to_left = pltpu.make_async_remote_copy(
            src_ref=source.at[level, part],
            dst_ref=from_right.at[sweep, level, part],
            send_sem=send_sem.at[sweep, level, c, 1],
            recv_sem=recv_sem.at[sweep, level, c, 1],
            device_id={"blk": left},
            device_id_type=MESH,
        )
        return to_right, to_left

    def terms(acc, cols, tiles, centre, sweep, level, source, m):
        base = (source * rows + m) * n
        low = from_left[sweep, source, m]
        mid = centre[source, m]
        high = from_right[sweep, source, m]
        for k in range(slots):
            column = cols[(level * rows + m) * slots + k]
            chosen = lax.select(column == base + right, high, jnp.zeros_like(high))
            chosen = lax.select(column == base + me, mid, chosen)
            chosen = lax.select(column == base + left, low, chosen)
            acc = acc - product(chosen, tiles[level, m, k])
        return acc

    load(0, 0).wait()
    y[0] = rhs_v[0].astype(jnp.bfloat16)
    pl.semaphore_wait(barrier, 2)
    for c in range(chunks):
        for copy in exchange(y, 0, 0, c):
            copy.start()

    def forward(level, carry):
        load(0, level).wait()
        load(1, level).wait()
        for c in range(chunks):
            for copy in exchange(y, 0, level - 1, c):
                copy.wait_recv()
            for m in range(c * step, (c + 1) * step):
                acc = terms(rhs_v[level, m], lower_cols, lower_v, y, 0, level, level - 1, m)
                y[level, m] = acc.astype(jnp.bfloat16)

            @pl.when(level < levels - 1)
            def _():
                for copy in exchange(y, 0, level, c):
                    copy.start()

        return carry

    lax.fori_loop(1, levels, forward, 0)

    last = levels - 1
    load(3, last).wait()
    for c in range(chunks):
        for m in range(c * step, (c + 1) * step):
            x[last, m] = product(y[last, m], inverse_v[last, m]).astype(jnp.bfloat16)
        for copy in exchange(x, 1, last, c):
            copy.start()

    def store(level):
        return pltpu.make_async_copy(x.at[level], out.at[level], store_sem.at[level])

    store(last).start()

    def backward(i, carry):
        level = last - 1 - i
        load(3, level).wait()
        load(2, level).wait()
        for c in range(chunks):
            for copy in exchange(x, 1, level + 1, c):
                copy.wait_recv()
            for m in range(c * step, (c + 1) * step):
                acc = terms(
                    y[level, m].astype(jnp.float32), upper_cols, upper_v, x, 1, level, level + 1, m
                )
                w = acc.astype(jnp.bfloat16)
                x[level, m] = product(w, inverse_v[level, m]).astype(jnp.bfloat16)

            @pl.when(level > 0)
            def _():
                for copy in exchange(x, 1, level, c):
                    copy.start()

        store(level).start()
        return carry

    lax.fori_loop(0, last, backward, 0)

    def finish(i, carry):
        for c in range(chunks):
            for copy in exchange(y, 0, i, c) + exchange(x, 1, i + 1, c):
                copy.wait_send()
        store(i).wait()
        return carry

    lax.fori_loop(0, last, finish, 0)
    store(last).wait()


def on_device(n, rhs, lower_tiles, lower_block_columns, upper_tiles, upper_cols, diag_inverse):
    rhs = rhs[:, :, 0]
    lower = lower_tiles[:, :, 0]
    upper = upper_tiles[:, :, 0]
    inverse = diag_inverse[:, :, 0]
    levels, rows, sides, block = rhs.shape
    chunks = CHUNKS if rows % CHUNKS == 0 else 1
    halo = pltpu.VMEM((2, levels, rows, sides, block), jnp.bfloat16)
    own = pltpu.VMEM((levels, rows, sides, block), jnp.bfloat16)
    any_space = pl.BlockSpec(memory_space=pl.ANY)
    small = pl.BlockSpec(memory_space=pltpu.SMEM)
    result = pl.pallas_call(
        functools.partial(sweep_kernel, n, chunks),
        out_shape=jax.ShapeDtypeStruct(rhs.shape, jnp.bfloat16),
        in_specs=[small, small, any_space, any_space, any_space, any_space],
        out_specs=any_space,
        scratch_shapes=[
            pltpu.VMEM(rhs.shape, rhs.dtype),
            pltpu.VMEM(lower.shape, lower.dtype),
            pltpu.VMEM(upper.shape, upper.dtype),
            pltpu.VMEM(inverse.shape, inverse.dtype),
            own,
            own,
            halo,
            halo,
            pltpu.SemaphoreType.DMA((4, levels)),
            pltpu.SemaphoreType.DMA((levels,)),
            pltpu.SemaphoreType.DMA((2, levels, chunks, 2)),
            pltpu.SemaphoreType.DMA((2, levels, chunks, 2)),
        ],
        compiler_params=pltpu.CompilerParams(collective_id=0, has_side_effects=True),
    )(
        lower_block_columns.reshape(-1),
        upper_cols.reshape(-1),
        rhs,
        lower,
        upper,
        inverse,
    )
    return result[:, :, None]


def solution(mesh):
    return jax.shard_map(
        functools.partial(on_device, mesh.shape["blk"]),
        mesh=mesh,
        in_specs=(
            P(None, None, "blk", "rhs", None),
            P(None, None, "blk", None, None, None),
            P(None, None, "blk", None),
            P(None, None, "blk", None, None, None),
            P(None, None, "blk", None),
            P(None, None, "blk", None, None),
        ),
        out_specs=P(None, None, "blk", "rhs", None),
        check_vma=False,
    )
```

time: 173 us -> 99.4 us (0.57)
  Pallas kernels: 0 us -> 93.7 us
  waiting for transfers between devices: 53.7 us -> 0 us
  starting transfers between devices: 34.2 us -> 0 us
  matrix products: 32.4 us -> 0 us
  local copies, waits for them, and re-layouts: 29.2 us -> 5.33 us
  other arithmetic: 12.7 us -> 0 us
  loops' own time: 9.5 us -> 0 us
    pallas_call x0 -> x1, Pallas kernels: none -> 93.7 us  [on_device(): pl.pallas_call(functools.partial(sweep_kernel, n, chunks), out_shape=jax....]
    ppermute x28 -> x0, waiting for transfers between devices: 53.7 us -> none  [the longest x14 39.2 us: extended(): lax.ppermute(lax.slice_in_dim(block, block.shape[dim] - width, None, axis...]
    ppermute x28 -> x0, starting transfers between devices: 34.2 us -> none  [the longest x14 26.2 us: extended(): lax.ppermute(lax.slice_in_dim(block, block.shape[dim] - width, None, axis...]
    dot_general x29 -> x0, matrix products: 32.4 us -> none  [the longest x8 13.7 us: apply_inverse(): jnp.einsum('vdj,voj->vdo', summed_terms, inverted_tile_matrix, preferred_...]
    slice x9 -> x0, local copies, waits for them, and re-layouts: 16.2 us -> none  [the longest x1 7.37 us: on_device(): lower_tile_group[1:]]
    another operation x2 -> x0, loops' own time: 9.5 us -> none  [the longest x1 4.84 us: on_device(): lax.scan(forward, first_level, (lower_tile_group[1:], lower_index[1:], si...]
    dynamic_slice x14 -> x0, local copies, waits for them, and re-layouts: 8.38 us -> none  [on_device(): lax.scan(forward, first_level, (lower_tile_group[1:], lower_index[1:], si...]
    add x14 -> x0, other arithmetic: 5.03 us -> none  [select_terms(): source = offset_step + (shift_amount_value + halo_width)]
  transfers between devices with their start and end apart: 28 -> 0, of which waited for: 27 -> 0; matrix products, arithmetic and copies ran while one was open for 12% -> 0% of each run, Pallas kernels for 0% -> 0%
where the time goes in v1:
time: 99.4 us; the launch traced here: 99.1 us
  Pallas kernels  93.7 us (94%)
  local copies, waits for them, and re-layouts  5.33 us (5%)
    pallas_call x1, Pallas kernels, on_device(): pl.pallas_call(functools.partial(sweep_kernel, n, chunks), out_shape=jax....  93.7 us
    unnamed x3, local copies, waits for them, and re-layouts  3.91 us

profile of v1, /device:TPU:0, one launch (start us, length us, event | category | flops | bytes accessed | tf_op | source)
XLA Modules:
  0.0 99.1 jit_solution(10529184466184725915)
XLA Ops:
  0.0 0.8 copy.8
  0.8 0.7 reshape.6.lower_cols
  1.5 0.8 copy.9
  2.3 0.7 reshape.7.upper_cols
  3.1 93.7 %shard_map.64 = bf16[8,8,64,128]{3,2,1,0:T(8,128)(2,1)} custom-call(s32[192]{0:T(256)} %reshape.6.lower_cols, s32[192]{0:T(256)} %reshape.7.upper_cols, f32[8,8,64,128]{3,2,1,0:T(8,128)} %bitcast.18, bf16[8,8,3,128,128]{4,3,2,1,0:T(8,128)(2,1)} %bitcast.15, bf16[8,8,3,128,128]{4,3,2,1,0:T(8,128)(2,1)} %bitcast.16, bf16[8,8,128,128]{3,2,1,0:T(8,128)(2,1)} %bitcast.19), custom_call_target="tpu_custom_call" | custom-call | tf_op jit(solution)/shard_map/pallas_call | solution.py:189
  96.8 2.3 %copy.12 = bf16[8,8,1,64,128]{4,3,2,1,0:T(8,128)(2,1)} copy(bf16[8,8,1,64,128]{4,3,2,1,0:T(8,128)(2,1)} %bitcast.17) | data formatting | bytes 2097152

commit v2 on v1

--- a/solution.py
+++ b/solution.py
@@ -9,6 +9,7 @@
 
 MESH = pl.DeviceIdType.MESH
 CHUNKS = 4
+LOOK = 2
 
 
 def product(x, tile):
@@ -31,8 +32,8 @@
     inverse_v,
     y,
     x,
-    from_left,
-    from_right,
+    from_near,
+    from_far,
     load_sem,
     store_sem,
     send_sem,
@@ -41,9 +42,15 @@
     levels, rows, sides, block = rhs.shape
     slots = lower.shape[2]
     step = rows // chunks
+    last = levels - 1
     me = lax.axis_index("blk")
-    left = lax.rem(me + n - 1, n)
-    right = lax.rem(me + 1, n)
+    odd = lax.rem(me, 2)
+    near = me + 1 - 2 * odd
+    far = lax.rem(me + 2 * odd + n - 1, n)
+    onward = me + 2 - 4 * odd
+    forwards = (onward >= 0) & (onward < n)
+    ends = (me == 0) | (me == n - 1)
+    feeder = lax.select(ends, far, me - 2 + 4 * odd)
 
     def load(kind, level):
         source, target = ((rhs, rhs_v), (lower, lower_v), (upper, upper_v), (inverse, inverse_v))[kind]
@@ -62,78 +69,101 @@
 
     load(0, 0).start()
     barrier = pltpu.get_barrier_semaphore()
-    for neighbour in (left, right):
-        pl.semaphore_signal(barrier, inc=1, device_id={"blk": neighbour}, device_id_type=MESH)
+    for device in (near, feeder):
+        pl.semaphore_signal(barrier, inc=1, device_id={"blk": device}, device_id_type=MESH)
     lax.fori_loop(1, levels, start_forward, 0)
     load(3, levels - 1).start()
     lax.fori_loop(0, levels - 1, start_backward, 0)
 
-    def exchange(source, sweep, level, c):
+    def remote(source, target, sweep, level, c, kind, device):
         part = pl.ds(c * step, step)
-        to_right = pltpu.make_async_remote_copy(
-            src_ref=source.at[level, part],
-            dst_ref=from_left.at[sweep, level, part],
-            send_sem=send_sem.at[sweep, level, c, 0],
-            recv_sem=recv_sem.at[sweep, level, c, 0],
-            device_id={"blk": right},
+        return pltpu.make_async_remote_copy(
+            src_ref=source.at[level, part] if kind != 1 else source.at[sweep, level, part],
+            dst_ref=target.at[sweep, level, part],
+            send_sem=send_sem.at[sweep, level, c, kind],
+            recv_sem=recv_sem.at[sweep, level, c, min(kind, 1)],
+            device_id={"blk": device},
             device_id_type=MESH,
         )
-        to_left = pltpu.make_async_remote_copy(
-            src_ref=source.at[level, part],
-            dst_ref=from_right.at[sweep, level, part],
-            send_sem=send_sem.at[sweep, level, c, 1],
-            recv_sem=recv_sem.at[sweep, level, c, 1],
-            device_id={"blk": left},
-            device_id_type=MESH,
-        )
-        return to_right, to_left
+
+    def to_near(own, sweep, level, c):
+        return remote(own, from_near, sweep, level, c, 0, near)
+
+    def to_onward(sweep, level, c):
+        return remote(from_near, from_far, sweep, level, c, 1, onward)
+
+    def to_far(own, sweep, level, c):
+        return remote(own, from_far, sweep, level, c, 2, far)
+
+    def send(own, sweep, level, c):
+        @pl.when(ends)
+        def _():
+            to_far(own, sweep, level, c).start()
+
+        to_near(own, sweep, level, c).start()
+
+    def relay(own, sweep, level, c):
+        to_near(own, sweep, level, c).wait_recv()
+
+        @pl.when(forwards)
+        def _():
+            to_onward(sweep, level, c).start()
+
+    def ahead(own, sweep, level, source, c):
+        if c + LOOK < chunks:
+            relay(own, sweep, source, c + LOOK)
+        else:
+
+            @pl.when((level > 0) & (level < last))
+            def _():
+                relay(own, sweep, level, c + LOOK - chunks)
 
     def terms(acc, cols, tiles, centre, sweep, level, source, m):
         base = (source * rows + m) * n
-        low = from_left[sweep, source, m]
+        side = from_near[sweep, source, m]
         mid = centre[source, m]
-        high = from_right[sweep, source, m]
+        other = from_far[sweep, source, m]
         for k in range(slots):
-            column = cols[(level * rows + m) * slots + k]
-            chosen = lax.select(column == base + right, high, jnp.zeros_like(high))
+            column = cols[level, k, 0, m]
+            chosen = lax.select(column == base + far, other, jnp.zeros_like(other))
             chosen = lax.select(column == base + me, mid, chosen)
-            chosen = lax.select(column == base + left, low, chosen)
+            chosen = lax.select(column == base + near, side, chosen)
             acc = acc - product(chosen, tiles[level, m, k])
         return acc
 
     load(0, 0).wait()
     y[0] = rhs_v[0].astype(jnp.bfloat16)
-    pl.semaphore_wait(barrier, 2)
+    pl.semaphore_wait(barrier, 1 + forwards.astype(jnp.int32) + ends.astype(jnp.int32))
     for c in range(chunks):
-        for copy in exchange(y, 0, 0, c):
-            copy.start()
+        send(y, 0, 0, c)
+    for c in range(LOOK):
+        relay(y, 0, 0, c)
 
     def forward(level, carry):
         load(0, level).wait()
         load(1, level).wait()
         for c in range(chunks):
-            for copy in exchange(y, 0, level - 1, c):
-                copy.wait_recv()
+            ahead(y, 0, level, level - 1, c)
+            to_far(y, 0, level - 1, c).wait_recv()
             for m in range(c * step, (c + 1) * step):
                 acc = terms(rhs_v[level, m], lower_cols, lower_v, y, 0, level, level - 1, m)
                 y[level, m] = acc.astype(jnp.bfloat16)
 
             @pl.when(level < levels - 1)
             def _():
-                for copy in exchange(y, 0, level, c):
-                    copy.start()
+                send(y, 0, level, c)
 
         return carry
 
     lax.fori_loop(1, levels, forward, 0)
 
-    last = levels - 1
     load(3, last).wait()
     for c in range(chunks):
         for m in range(c * step, (c + 1) * step):
             x[last, m] = product(y[last, m], inverse_v[last, m]).astype(jnp.bfloat16)
-        for copy in exchange(x, 1, last, c):
-            copy.start()
+        send(x, 1, last, c)
+    for c in range(LOOK):
+        relay(x, 1, last, c)
 
     def store(level):
         return pltpu.make_async_copy(x.at[level], out.at[level], store_sem.at[level])
@@ -145,8 +175,8 @@
         load(3, level).wait()
         load(2, level).wait()
         for c in range(chunks):
-            for copy in exchange(x, 1, level + 1, c):
-                copy.wait_recv()
+            ahead(x, 1, level, level + 1, c)
+            to_far(x, 1, level + 1, c).wait_recv()
             for m in range(c * step, (c + 1) * step):
                 acc = terms(
                     y[level, m].astype(jnp.float32), upper_cols, upper_v, x, 1, level, level + 1, m
@@ -156,8 +186,7 @@
 
             @pl.when(level > 0)
             def _():
-                for copy in exchange(x, 1, level, c):
-                    copy.start()
+                send(x, 1, level, c)
 
         store(level).start()
         return carry
@@ -166,8 +195,17 @@
 
     def finish(i, carry):
         for c in range(chunks):
-            for copy in exchange(y, 0, i, c) + exchange(x, 1, i + 1, c):
-                copy.wait_send()
+            for own, sweep, level in ((y, 0, i), (x, 1, i + 1)):
+                to_near(own, sweep, level, c).wait_send()
+
+                @pl.when(forwards)
+                def _():
+                    to_onward(sweep, level, c).wait_send()
+
+                @pl.when(ends)
+                def _():
+                    to_far(own, sweep, level, c).wait_send()
+
         store(i).wait()
         return carry
 
@@ -202,13 +240,13 @@
             halo,
             pltpu.SemaphoreType.DMA((4, levels)),
             pltpu.SemaphoreType.DMA((levels,)),
-            pltpu.SemaphoreType.DMA((2, levels, chunks, 2)),
+            pltpu.SemaphoreType.DMA((2, levels, chunks, 3)),
             pltpu.SemaphoreType.DMA((2, levels, chunks, 2)),
         ],
         compiler_params=pltpu.CompilerParams(collective_id=0, has_side_effects=True),
     )(
-        lower_block_columns.reshape(-1),
-        upper_cols.reshape(-1),
+        lower_block_columns.transpose(0, 3, 2, 1),
+        upper_cols.transpose(0, 3, 2, 1),
         rhs,
         lower,
         upper,

time: 99.4 us -> 124 us (1.25)
  Pallas kernels: 93.7 us -> 121 us
  local copies, waits for them, and re-layouts: 5.33 us -> 2.26 us
    pallas_call x1, Pallas kernels: 93.7 us -> 121 us  [on_device(): pl.pallas_call(functools.partial(sweep_kernel, n, chunks), out_shape=jax....]
    unnamed x3 -> x1, local copies, waits for them, and re-layouts: 3.91 us -> 2.26 us
    reshape x2 -> x0, local copies, waits for them, and re-layouts: 1.43 us -> none  [the longest x1 0.73 us: on_device(): upper_cols.reshape(-1)]
where the time goes in v2:
time: 124 us
  Pallas kernels  121 us (98%)
  local copies, waits for them, and re-layouts  2.26 us (2%)
    pallas_call x1, Pallas kernels, on_device(): pl.pallas_call(functools.partial(sweep_kernel, n, chunks), out_shape=jax....  121 us

profile of v2, /device:TPU:0, one launch (start us, length us, event | category | flops | bytes accessed | tf_op | source)
XLA Modules:
  0.0 123.5 jit_solution(2579238730687047213)
XLA Ops:
  0.0 121.3 %shard_map.64 = bf16[8,8,64,128]{3,2,1,0:T(8,128)(2,1)} custom-call(s32[8,3,1,8]{3,2,1,0:T(1,128)} %bitcast.14, s32[8,3,1,8]{3,2,1,0:T(1,128)} %bitcast.15, f32[8,8,64,128]{3,2,1,0:T(8,128)} %bitcast.12, bf16[8,8,3,128,128]{4,3,2,1,0:T(8,128)(2,1)} %bitcast.9, bf16[8,8,3,128,128]{4,3,2,1,0:T(8,128)(2,1)} %bitcast.10, bf16[8,8,128,128]{3,2,1,0:T(8,128)(2,1)} %bitcast.13), custom_call_target="tpu_custom_call" | custom-call | tf_op jit(solution)/shard_map/pallas_call | solution.py:227
  121.3 2.3 %copy.9 = bf16[8,8,1,64,128]{4,3,2,1,0:T(8,128)(2,1)} copy(bf16[8,8,1,64,128]{4,3,2,1,0:T(8,128)(2,1)} %bitcast.11) | data formatting | bytes 2097152

commit v3 on v2

--- a/solution.py
+++ b/solution.py
@@ -8,8 +8,8 @@
 from jax.sharding import PartitionSpec as P
 
 MESH = pl.DeviceIdType.MESH
-CHUNKS = 4
-LOOK = 2
+CHUNKS = 8
+RELAYED = 1
 
 
 def product(x, tile):
@@ -47,10 +47,8 @@
     odd = lax.rem(me, 2)
     near = me + 1 - 2 * odd
     far = lax.rem(me + 2 * odd + n - 1, n)
-    onward = me + 2 - 4 * odd
-    forwards = (onward >= 0) & (onward < n)
-    ends = (me == 0) | (me == n - 1)
-    feeder = lax.select(ends, far, me - 2 + 4 * odd)
+    onward = lax.rem(me + 2 - 4 * odd + n, n)
+    feeder = lax.rem(me - 2 + 4 * odd + n, n)
 
     def load(kind, level):
         source, target = ((rhs, rhs_v), (lower, lower_v), (upper, upper_v), (inverse, inverse_v))[kind]
@@ -69,54 +67,47 @@
 
     load(0, 0).start()
     barrier = pltpu.get_barrier_semaphore()
-    for device in (near, feeder):
+    for device in (near, far, feeder) if RELAYED else (near, far):
         pl.semaphore_signal(barrier, inc=1, device_id={"blk": device}, device_id_type=MESH)
     lax.fori_loop(1, levels, start_forward, 0)
     load(3, levels - 1).start()
     lax.fori_loop(0, levels - 1, start_backward, 0)
 
-    def remote(source, target, sweep, level, c, kind, device):
-        part = pl.ds(c * step, step)
+    def group(turn, j):
+        return lax.rem(turn * RELAYED + j, chunks) * step
+
+    def remote(source, target, sweep, level, turn, j, kind, device):
         return pltpu.make_async_remote_copy(
-            src_ref=source.at[level, part] if kind != 1 else source.at[sweep, level, part],
-            dst_ref=target.at[sweep, level, part],
-            send_sem=send_sem.at[sweep, level, c, kind],
-            recv_sem=recv_sem.at[sweep, level, c, min(kind, 1)],
+            src_ref=source.at[level, pl.ds(group(turn, j), step)],
+            dst_ref=target.at[sweep, level, pl.ds(group(turn, j), step)],
+            send_sem=send_sem.at[sweep, level, j, kind],
+            recv_sem=recv_sem.at[sweep, level, j, kind],
             device_id={"blk": device},
             device_id_type=MESH,
         )
 
-    def to_near(own, sweep, level, c):
-        return remote(own, from_near, sweep, level, c, 0, near)
-
-    def to_onward(sweep, level, c):
-        return remote(from_near, from_far, sweep, level, c, 1, onward)
-
-    def to_far(own, sweep, level, c):
-        return remote(own, from_far, sweep, level, c, 2, far)
-
-    def send(own, sweep, level, c):
-        @pl.when(ends)
-        def _():
-            to_far(own, sweep, level, c).start()
-
-        to_near(own, sweep, level, c).start()
-
-    def relay(own, sweep, level, c):
-        to_near(own, sweep, level, c).wait_recv()
-
-        @pl.when(forwards)
-        def _():
-            to_onward(sweep, level, c).start()
-
-    def ahead(own, sweep, level, source, c):
-        if c + LOOK < chunks:
-            relay(own, sweep, source, c + LOOK)
-        else:
-
-            @pl.when((level > 0) & (level < last))
-            def _():
-                relay(own, sweep, level, c + LOOK - chunks)
+    def to_near(own, sweep, level, turn, j):
+        return remote(own, from_near, sweep, level, turn, j, 0, near)
+
+    def to_far(own, sweep, level, turn, j):
+        if j < RELAYED:
+            return remote(from_near.at[sweep], from_far, sweep, level, turn, j, 1, onward)
+        return remote(own, from_far, sweep, level, turn, j, 1, far)
+
+    def send(own, sweep, level, turn, j):
+        if j >= RELAYED:
+            to_far(own, sweep, level, turn, j).start()
+        to_near(own, sweep, level, turn, j).start()
+
+    def relay(own, sweep, level, turn):
+        for j in range(RELAYED):
+            to_near(own, sweep, level, turn, j).wait_recv()
+            to_far(own, sweep, level, turn, j).start()
+
+    def receive(own, sweep, level, turn, j):
+        if j >= RELAYED:
+            to_near(own, sweep, level, turn, j).wait_recv()
+        to_far(own, sweep, level, turn, j).wait_recv()
 
     def terms(acc, cols, tiles, centre, sweep, level, source, m):
         base = (source * rows + m) * n
@@ -133,51 +124,53 @@
 
     load(0, 0).wait()
     y[0] = rhs_v[0].astype(jnp.bfloat16)
-    pl.semaphore_wait(barrier, 1 + forwards.astype(jnp.int32) + ends.astype(jnp.int32))
-    for c in range(chunks):
-        send(y, 0, 0, c)
-    for c in range(LOOK):
-        relay(y, 0, 0, c)
+    pl.semaphore_wait(barrier, 3 if RELAYED else 2)
+    for j in range(chunks):
+        send(y, 0, 0, 0, j)
+    relay(y, 0, 0, 0)
 
     def forward(level, carry):
         load(0, level).wait()
         load(1, level).wait()
-        for c in range(chunks):
-            ahead(y, 0, level, level - 1, c)
-            to_far(y, 0, level - 1, c).wait_recv()
-            for m in range(c * step, (c + 1) * step):
+        for j in range(chunks):
+            receive(y, 0, level - 1, level - 1, (j + RELAYED) % chunks)
+            for i in range(step):
+                m = group(level, j) + i
                 acc = terms(rhs_v[level, m], lower_cols, lower_v, y, 0, level, level - 1, m)
                 y[level, m] = acc.astype(jnp.bfloat16)
 
-            @pl.when(level < levels - 1)
+            @pl.when(level < last)
             def _():
-                send(y, 0, level, c)
+                send(y, 0, level, level, j)
+
+        @pl.when(level < last)
+        def _():
+            relay(y, 0, level, level)
 
         return carry
 
     lax.fori_loop(1, levels, forward, 0)
-
-    load(3, last).wait()
-    for c in range(chunks):
-        for m in range(c * step, (c + 1) * step):
-            x[last, m] = product(y[last, m], inverse_v[last, m]).astype(jnp.bfloat16)
-        send(x, 1, last, c)
-    for c in range(LOOK):
-        relay(x, 1, last, c)
 
     def store(level):
         return pltpu.make_async_copy(x.at[level], out.at[level], store_sem.at[level])
 
+    load(3, last).wait()
+    for j in range(chunks):
+        for i in range(step):
+            m = group(0, j) + i
+            x[last, m] = product(y[last, m], inverse_v[last, m]).astype(jnp.bfloat16)
+        send(x, 1, last, 0, j)
     store(last).start()
-
-    def backward(i, carry):
-        level = last - 1 - i
+    relay(x, 1, last, 0)
+
+    def backward(turn, carry):
+        level = last - turn
         load(3, level).wait()
         load(2, level).wait()
-        for c in range(chunks):
-            ahead(x, 1, level, level + 1, c)
-            to_far(x, 1, level + 1, c).wait_recv()
-            for m in range(c * step, (c + 1) * step):
+        for j in range(chunks):
+            receive(x, 1, level + 1, turn - 1, (j + RELAYED) % chunks)
+            for i in range(step):
+                m = group(turn, j) + i
                 acc = terms(
                     y[level, m].astype(jnp.float32), upper_cols, upper_v, x, 1, level, level + 1, m
                 )
@@ -186,27 +179,24 @@
 
             @pl.when(level > 0)
             def _():
-                send(x, 1, level, c)
+                send(x, 1, level, turn, j)
 
         store(level).start()
-        return carry
-
-    lax.fori_loop(0, last, backward, 0)
-
-    def finish(i, carry):
-        for c in range(chunks):
-            for own, sweep, level in ((y, 0, i), (x, 1, i + 1)):
-                to_near(own, sweep, level, c).wait_send()
-
-                @pl.when(forwards)
-                def _():
-                    to_onward(sweep, level, c).wait_send()
-
-                @pl.when(ends)
-                def _():
-                    to_far(own, sweep, level, c).wait_send()
-
-        store(i).wait()
+
+        @pl.when(level > 0)
+        def _():
+            relay(x, 1, level, turn)
+
+        return carry
+
+    lax.fori_loop(1, levels, backward, 0)
+
+    def finish(turn, carry):
+        for j in range(chunks):
+            for own, sweep, level in ((y, 0, turn), (x, 1, last - turn)):
+                to_near(own, sweep, level, turn, j).wait_send()
+                to_far(own, sweep, level, turn, j).wait_send()
+        store(turn).wait()
         return carry
 
     lax.fori_loop(0, last, finish, 0)
@@ -240,7 +230,7 @@
             halo,
             pltpu.SemaphoreType.DMA((4, levels)),
             pltpu.SemaphoreType.DMA((levels,)),
-            pltpu.SemaphoreType.DMA((2, levels, chunks, 3)),
+            pltpu.SemaphoreType.DMA((2, levels, chunks, 2)),
             pltpu.SemaphoreType.DMA((2, levels, chunks, 2)),
         ],
         compiler_params=pltpu.CompilerParams(collective_id=0, has_side_effects=True),

time: 124 us -> 94 us (0.76)
  Pallas kernels: 121 us -> 91.4 us
    pallas_call x1, Pallas kernels: 121 us -> 91.4 us  [on_device(): pl.pallas_call(functools.partial(sweep_kernel, n, chunks), out_shape=jax....]
where the time goes in v3:
time: 94 us; the launch traced here: 93.7 us
  Pallas kernels  91.4 us (97%)
  local copies, waits for them, and re-layouts  2.26 us (2%)
    pallas_call x1, Pallas kernels, on_device(): pl.pallas_call(functools.partial(sweep_kernel, n, chunks), out_shape=jax....  91.4 us
    unnamed x1, local copies, waits for them, and re-layouts  2.26 us

profile of v3, /device:TPU:0, one launch (start us, length us, event | category | flops | bytes accessed | tf_op | source)
XLA Modules:
  0.0 93.7 jit_solution(10917090183187166926)
XLA Ops:
  0.0 91.4 %shard_map.64 = bf16[8,8,64,128]{3,2,1,0:T(8,128)(2,1)} custom-call(s32[8,3,1,8]{3,2,1,0:T(1,128)} %bitcast.14, s32[8,3,1,8]{3,2,1,0:T(1,128)} %bitcast.15, f32[8,8,64,128]{3,2,1,0:T(8,128)} %bitcast.12, bf16[8,8,3,128,128]{4,3,2,1,0:T(8,128)(2,1)} %bitcast.9, bf16[8,8,3,128,128]{4,3,2,1,0:T(8,128)(2,1)} %bitcast.10, bf16[8,8,128,128]{3,2,1,0:T(8,128)(2,1)} %bitcast.13), custom_call_target="tpu_custom_call" | custom-call | tf_op jit(solution)/shard_map/pallas_call | solution.py:217
  91.4 2.3 %copy.9 = bf16[8,8,1,64,128]{4,3,2,1,0:T(8,128)(2,1)} copy(bf16[8,8,1,64,128]{4,3,2,1,0:T(8,128)(2,1)} %bitcast.11) | data formatting | bytes 2097152

commit v4 on v3

--- a/solution.py
+++ b/solution.py
@@ -9,6 +9,7 @@
 
 MESH = pl.DeviceIdType.MESH
 CHUNKS = 8
+VMEM_LIMIT = 52 * 2**20
 RELAYED = 1
 
 
@@ -95,9 +96,9 @@
         return remote(own, from_far, sweep, level, turn, j, 1, far)
 
     def send(own, sweep, level, turn, j):
+        to_near(own, sweep, level, turn, j).start()
         if j >= RELAYED:
             to_far(own, sweep, level, turn, j).start()
-        to_near(own, sweep, level, turn, j).start()
 
     def relay(own, sweep, level, turn):
         for j in range(RELAYED):
@@ -233,7 +234,7 @@
             pltpu.SemaphoreType.DMA((2, levels, chunks, 2)),
             pltpu.SemaphoreType.DMA((2, levels, chunks, 2)),
         ],
-        compiler_params=pltpu.CompilerParams(collective_id=0, has_side_effects=True),
+        compiler_params=pltpu.CompilerParams(collective_id=0, has_side_effects=True, vmem_limit_bytes=VMEM_LIMIT),
     )(
         lower_block_columns.transpose(0, 3, 2, 1),
         upper_cols.transpose(0, 3, 2, 1),

time: 94 us -> 93.6 us (level)
    unnamed x1 -> x5, local copies, waits for them, and re-layouts: 2.26 us -> 2.39 us
where the time goes in v4:
time: 93.6 us; the launch traced here: 93.2 us
  Pallas kernels  90.8 us (97%)
  local copies, waits for them, and re-layouts  2.39 us (3%)
    pallas_call x1, Pallas kernels, on_device(): pl.pallas_call(functools.partial(sweep_kernel, n, chunks), out_shape=jax....  90.8 us
    unnamed x5, local copies, waits for them, and re-layouts  2.39 us

profile of v4, /device:TPU:0, one launch (start us, length us, event | category | flops | bytes accessed | tf_op | source)
XLA Modules:
  0.0 93.2 jit_solution(15063075146530187091)
XLA Ops:
  0.0 0.0 copy-start
  0.0 0.7 copy-done
  0.7 0.0 copy-start.1
  0.7 0.7 copy-done.1
  1.4 90.8 %shard_map.64 = bf16[8,8,64,128]{3,2,1,0:T(8,128)(2,1)S(1)} custom-call(s32[8,3,1,8]{3,2,1,0:T(1,128)S(1)} %bitcast.10, s32[8,3,1,8]{3,2,1,0:T(1,128)S(1)} %bitcast.11, f32[8,8,64,128]{3,2,1,0:T(8,128)} %bitcast.14, bf16[8,8,3,128,128]{4,3,2,1,0:T(8,128)(2,1)} %bitcast.12, bf16[8,8,3,128,128]{4,3,2,1,0:T(8,128)(2,1)} %bitcast.13, ...), custom_call_target="tpu_custom_call" | custom-call | tf_op jit(solution)/shard_map/pallas_call | solution.py:218
  92.3 1.0 %copy.9 = bf16[8,8,1,64,128]{4,3,2,1,0:T(8,128)(2,1)} copy(bf16[8,8,1,64,128]{4,3,2,1,0:T(8,128)(2,1)S(1)} %bitcast.9) | data formatting | bytes 2097152
Async XLA Ops:
  0.0 0.7 copy-start
  0.7 0.7 copy-start.1
